TPU v7x, 32 devices: a whole 2x2x4 slice. The times are simulated.
32 devices in a mesh: tp: 4 (over y, x), row: 4 (over z), col: 2 (over core).
Axes of the slice: x: 2, y: 2, z: 4, core: 2. Of those that a mesh axis runs over, the one named last changes fastest.
Arguments:
- hidden: bfloat16 [128, 14336], P('col', 'row'), may hold values from -6 to 6
- out_grad: bfloat16 [128, 4096], P(None, ('tp', 'row')), may hold values from -6 to 6
- basis_in: bfloat16 [14336, 4096], P(('row', 'col'), 'tp'), may hold values from -0.046875 to 0.046875
- basis_out: bfloat16 [4096, 1024], P(('tp', 'row'), 'col'), may hold values from -0.09375 to 0.09375
- eigen: float32 [4096, 1024], P(('tp', 'row'), 'col'), may hold values from 0.02 to 2
Outputs:
- precond: float32 [4096, 14336], P(('tp', 'col'), 'row')
All inputs are finite; a program needn't handle non-finite values.
Results may differ from a plain program's by a relative error of at most 0.024.
Values may be sent and summed in bfloat16 or wider, within the bound.
No kernel may reach another device: no remote copies, remote signals or barrier semaphores. Data moves between devices by JAX's collectives and lax.ppermute only.
A program may use at most 64 MiB of HBM per device.

v0:
```python
import jax
import jax.numpy as jnp
from jax import lax
from jax.sharding import PartitionSpec as P

damping = 0.01


def contract_rows(left, right):
    return lax.dot_general(
        left, right, (((0,), (0,)), ((), ())), preferred_element_type=jnp.float32
    )


def contract_cols(left, right):
    return lax.dot_general(
        left, right, (((1,), (1,)), ((), ())), preferred_element_type=jnp.float32
    )


def shards(hidden, out_grad, basis_in, basis_out, eigen):
    tp_count = lax.axis_size("tp")
    col_count = lax.axis_size("col")
    basis_block = lax.all_gather(basis_in, "col", axis=0, tiled=True)
    partial_in = jnp.dot(hidden, basis_block, preferred_element_type=jnp.float32)
    rotated_in = lax.psum_scatter(
        partial_in.astype(jnp.bfloat16), "row", scatter_dimension=1, tiled=True
    )
    rotated_in = lax.all_gather(rotated_in, "col", axis=0, tiled=True)
    queries = rotated_in.shape[0]
    partial_out = jnp.dot(out_grad, basis_out, preferred_element_type=jnp.float32)
    rotated_out = lax.psum(partial_out, ("tp", "row")).astype(jnp.bfloat16)
    coeff = contract_rows(rotated_in, rotated_out)
    scaled = (coeff / (queries * (eigen + damping))).astype(jnp.bfloat16)
    mixed_part = contract_cols(scaled, lax.all_gather(basis_out, ("tp", "row"), axis=0, tiled=True))
    depth = mixed_part.shape[0]
    width = mixed_part.shape[1]
    mixed_part = mixed_part.reshape(depth, tp_count, col_count, width // (tp_count * col_count))
    mixed = lax.psum_scatter(
        mixed_part.astype(jnp.bfloat16), "col", scatter_dimension=2, tiled=True
    ).astype(jnp.float32)
    mixed = mixed.reshape(depth, width // col_count).astype(jnp.bfloat16)
    mixed = lax.all_gather(mixed, "row", axis=0, tiled=True)
    return lax.psum_scatter(
        lax.dot_general(
            mixed, basis_block, (((0,), (1,)), ((), ())), preferred_element_type=jnp.float32
        ).astype(jnp.bfloat16),
        "tp",
        scatter_dimension=0,
        tiled=True,
    ).astype(jnp.float32)


def solution(mesh):
    placed = (
        P("col", "row"),
        P(None, ("tp", "row")),
        P(("row", "col"), "tp"),
        P(("tp", "row"), "col"),
        P(("tp", "row"), "col"),
    )
    return jax.shard_map(
        shards, mesh=mesh, in_specs=placed, out_specs=P(("tp", "col"), "row"), check_vma=False
    )
```

profile of v0, /device:TPU:0, one launch (start us, length us, event | category | flops | bytes accessed | tf_op | source)
XLA Modules:
  0.0 397.8 jit_solution(9604397828768367093)
XLA Ops:
  7.4 0.0 copy-start
  7.4 0.0 all-gather.4.cloned.1.call-start
  7.4 0.7 all-gather.4.cloned.1.call-update
  8.1 0.0 copy-start.1
  8.1 0.0 copy-start.2
  8.1 0.0 copy-start.3
  8.1 0.0 reduce-scatter.4.cloned.1.call-start
  8.2 22.6 %all-gather.4.cloned.1.call-done = bf16[3584,1024]{1,0:T(8,128)(2,1)} async-done(((bf16[1792,1024]{1,0:T(8,128)(2,1)}), bf16[3584,1024]{1,0:T(8,128)(2,1)}) %all-gather.4.cloned.1.call-update) | async-done | bytes 7340048 | tf_op jit(solution)/shard_map/all_gather | solution.py:24
  30.8 0.0 copy-done
  30.8 5.1 %convolution_convert_fusion.2 = bf16[64,1024]{1,0:T(8,128)(2,1)} fusion(bf16[64,3584]{1,0:T(8,128)(2,1)S(1)} %copy-done, bf16[3584,1024]{1,0:T(8,128)(2,1)} %all-gather.4.cloned.1.call-done), kind=kOutput, calls=%fused_computation.4 | convolution fusion | flops 469827584 | bytes 7929856 | tf_op jit(solution)/shard_map/dot_general | solution.py:25
  35.9 0.0 reduce-scatter.4.cloned.1.call-update
  35.9 0.0 all-gather.6.cloned.1.call-start
  36.0 0.5 all-gather.6.cloned.1.call-update
  36.5 0.0 reduce-scatter.6.cloned.1.call-start
  36.5 0.0 copy-done.1
  36.6 0.0 copy-done.2
  36.6 0.2 fusion.9
  36.8 85.1 %all-reduce.1 = bf16[128,512]{1,0:T(8,128)(2,1)S(1)} all-reduce(f32[128,512]{1,0:T(8,128)S(1)} %fusion.9), channel_id=1, replica_groups=mesh['tp'=4,'row'=4,'col'=2] {'tp','row'}, use_global_device_ids=true, to_apply=%region_1.0 | all-reduce | flops 65536 | bytes 393216 | tf_op jit(solution)/shard_map/psum | solution.py:32
  121.9 0.0 reduce-scatter.4.cloned.1.call-done
  121.9 2.1 all_gather.13
  124.0 0.0 all-gather.6.cloned.1.call-done
  124.0 0.0 copy-done.3
  124.0 4.9 %convolution_convert_fusion.1 = bf16[256,4096]{1,0:T(8,128)(2,1)} fusion(bf16[4096,512]{1,0:T(8,128)(2,1)} %all-gather.6.cloned.1.call-done, bf16[128,256]{1,0:T(8,128)(2,1)S(1)} %all_gather.13, f32[256,512]{1,0:T(8,128)S(1)} %copy-done.3, bf16[128,512]{1,0:T(8,128)(2,1)S(1)} %all-reduce.1), kind=kOutput, calls=%fused_computation.1 | convolution fusion | flops 1108869120 | bytes 7012352 | tf_op jit(solution)/shard_map/dot_general | solution.py:16
  128.9 3.3 convert_element_type.30
  132.2 4.1 %copy.6 = bf16[256,4,2,512]{0,3,1,2:T(8,128)(2,1)} copy(bf16[256,4,2,512]{3,2,1,0:T(2,128)(2,1)S(1)} %convert_element_type.30) | data formatting | bytes 4194304 | tf_op jit(solution)/shard_map/convert_element_type | solution.py:40
  136.3 0.0 reduce-scatter.6.cloned.1.call-update
  136.4 0.0 all-gather.8.cloned.1.call-start
  136.4 6.9 %reduce-scatter.6.cloned.1.call-done = bf16[256,4,1,512]{0,3,1,2:T(8,128)(2,1)} async-done(((bf16[256,4,2,512]{0,3,1,2:T(8,128)(2,1)}), bf16[256,4,1,512]{0,3,1,2:T(8,128)(2,1)}) %reduce-scatter.6.cloned.1.call-update) | async-done | bytes 1048592 | tf_op jit(solution)/shard_map/reduce_scatter | solution.py:39
  143.3 0.0 all-gather.8.cloned.1.call-update
  143.4 0.0 reduce-scatter.8.cloned.1.call-start
  143.4 83.2 %all-gather.8.cloned.1.call-done = bf16[1024,2048]{0,1:T(8,128)(2,1)} async-done(((bf16[256,2048]{0,1:T(8,128)(2,1)}), bf16[1024,2048]{0,1:T(8,128)(2,1)}) %all-gather.8.cloned.1.call-update) | async-done | bytes 4194320 | tf_op jit(solution)/shard_map/all_gather | solution.py:43
  226.6 22.0 %convolution_convert_fusion = bf16[2048,3584]{1,0:T(8,128)(2,1)} fusion(bf16[1024,2048]{0,1:T(8,128)(2,1)} %all-gather.8.cloned.1.call-done, bf16[3584,1024]{1,0:T(8,128)(2,1)} %all-gather.4.cloned.1.call-done), kind=kOutput, calls=%fused_computation | convolution fusion | flops 15039725568 | bytes 26214400 | tf_op jit(solution)/shard_map/dot_general | solution.py:45
  248.6 0.0 reduce-scatter.8.cloned.1.call-update
  248.7 135.9 %reduce-scatter.8.cloned.1.call-done = bf16[512,3584]{1,0:T(8,128)(2,1)} async-done(((bf16[2048,3584]{1,0:T(8,128)(2,1)}), bf16[512,3584]{1,0:T(8,128)(2,1)}) %reduce-scatter.8.cloned.1.call-update) | async-done | bytes 3670032 | tf_op jit(solution)/shard_map/reduce_scatter | solution.py:44
  384.6 6.0 %convert_element_type.33 = f32[512,3584]{1,0:T(8,128)} convert(bf16[512,3584]{1,0:T(8,128)(2,1)} %reduce-scatter.8.cloned.1.call-done) | non-fusion elementwise | flops 1835008 | bytes 11010048 | tf_op jit(solution)/shard_map/convert_element_type | solution.py:51
Async XLA Ops:
  7.4 23.4 %copy-start = (bf16[64,3584]{1,0:T(8,128)(2,1)S(1)}, bf16[64,3584]{1,0:T(8,128)(2,1)}, u32[]{:S(2)}) copy-start(bf16[64,3584]{1,0:T(8,128)(2,1)} %param.5) | copy-start | bytes 1376260
  7.4 23.4 %all-gather.4.cloned.1.call-start = ((), (), s32[]{:S(2)}) async-start(), calls=%async_computation.3 | async-start | bytes 11010048 | tf_op jit(solution)/shard_map/all_gather | solution.py:24
  8.1 28.5 %copy-start.1 = (bf16[256,512]{1,0:T(8,128)(2,1)S(1)}, bf16[256,512]{1,0:T(8,128)(2,1)}, u32[]{:S(2)}) copy-start(bf16[256,512]{1,0:T(8,128)(2,1)} %param.8) | copy-start | bytes 786436
  8.1 28.5 %copy-start.2 = (bf16[128,256]{1,0:T(8,128)(2,1)S(1)}, bf16[128,256]{1,0:T(8,128)(2,1)}, u32[]{:S(2)}) copy-start(bf16[128,256]{1,0:T(8,128)(2,1)} %param.6) | copy-start | bytes 196612
  8.1 115.9 %copy-start.3 = (f32[256,512]{1,0:T(8,128)S(1)}, f32[256,512]{1,0:T(8,128)}, u32[]{:S(2)}) copy-start(f32[256,512]{1,0:T(8,128)} %param.9) | copy-start | bytes 1572868
  8.1 113.8 %reduce-scatter.4.cloned.1.call-start = ((), (), s32[]{:S(2)}) async-start(), calls=%async_computation.4 | async-start | bytes 163840 | tf_op jit(solution)/shard_map/reduce_scatter | solution.py:26
  35.9 88.1 %all-gather.6.cloned.1.call-start = ((), (), s32[]{:S(2)}) async-start(), calls=%async_computation.5 | async-start | bytes 4456448 | tf_op jit(solution)/shard_map/all_gather | solution.py:35
  36.5 106.8 %reduce-scatter.6.cloned.1.call-start = ((), (), s32[]{:S(2)}) async-start(), calls=%async_computation.6 | async-start | bytes 3145728 | tf_op jit(solution)/shard_map/reduce_scatter | solution.py:39
  136.4 90.2 %all-gather.8.cloned.1.call-start = ((), (), s32[]{:S(2)}) async-start(), calls=%async_computation.7 | async-start | bytes 5242880 | tf_op jit(solution)/shard_map/all_gather | solution.py:43
  143.4 241.2 %reduce-scatter.8.cloned.1.call-start = ((), (), s32[]{:S(2)}) async-start(), calls=%async_computation.8 | async-start | bytes 18350080 | tf_op jit(solution)/shard_map/reduce_scatter | solution.py:44
Sparse Core Ops, SparseCore 0:
  9.7 21.0 all-gather.3
  36.0 21.2 reduce-scatter.3
  136.5 6.8 reduce-scatter.5
  144.7 81.7 all-gather.7
Sparse Core Ops, SparseCore 1:
  39.2 78.1 all-gather.5
  248.7 135.8 reduce-scatter.7
where the time goes:
time: 398 us
  waiting for transfers between devices  250 us (63%)
  blocking collectives  87.2 us (22%)
  matrix products  32.3 us (8%)
  between operations  14.7 us (4%)
  local copies, waits for them, and re-layouts  7.4 us (2%)
  other arithmetic  6.04 us (2%)
    reduce_scatter x1, waiting for transfers between devices, shards(): lax.psum_scatter(lax.dot_general(mixed, basis_block, (((0,), (1,)), ((),...  136 us
    psum x1, blocking collectives, shards(): rotated_out = lax.psum(partial_out, ('tp', 'row')).astype(jnp.bfloat16)  85.1 us
    all_gather x1, waiting for transfers between devices, shards(): mixed = lax.all_gather(mixed, 'row', axis=0, tiled=True)  83.2 us
    all_gather x1, waiting for transfers between devices, shards(): basis_block = lax.all_gather(basis_in, 'col', axis=0, tiled=True)  22.6 us
    dot_general x1, matrix products, shards(): lax.dot_general(mixed, basis_block, (((0,), (1,)), ((), ())), preferred_e...  22 us
  transfers between devices with their start and end apart: 6, of which 4 were waited for; matrix products, arithmetic and copies ran while one was open for 0% of the time, Pallas kernels for 0%

commit v1 on v0

--- a/solution.py
+++ b/solution.py
@@ -19,6 +19,12 @@
 
 
 def shards(hidden, out_grad, basis_in, basis_out, eigen):
+
+    def expand_skins_in(array_here):
+        for dev_i in ("tp", "row"):
+            array_here = jax.lax.psum(array_here, dev_i)
+        return array_here
+
     tp_count = lax.axis_size("tp")
     col_count = lax.axis_size("col")
     basis_block = lax.all_gather(basis_in, "col", axis=0, tiled=True)
@@ -29,7 +35,7 @@
     rotated_in = lax.all_gather(rotated_in, "col", axis=0, tiled=True)
     queries = rotated_in.shape[0]
     partial_out = jnp.dot(out_grad, basis_out, preferred_element_type=jnp.float32)
-    rotated_out = lax.psum(partial_out, ("tp", "row")).astype(jnp.bfloat16)
+    rotated_out = expand_skins_in(partial_out).astype(jnp.bfloat16)
     coeff = contract_rows(rotated_in, rotated_out)
     scaled = (coeff / (queries * (eigen + damping))).astype(jnp.bfloat16)
     mixed_part = contract_cols(scaled, lax.all_gather(basis_out, ("tp", "row"), axis=0, tiled=True))

time: 398 us -> 412 us (1.035)
  waiting for transfers between devices: 250 us -> 321 us
  blocking collectives: 87.2 us -> 27.7 us
    psum x1, blocking collectives: 85.1 us -> 25.6 us  [expand_skins_in(): array_here = jax.lax.psum(array_here, dev_i)]
    all_gather x1, waiting for transfers between devices: 0.01 us -> 51.4 us  [shards(): lax.all_gather(basis_out, ('tp', 'row'), axis=0, tiled=True)]
    psum x0 -> x1, waiting for transfers between devices: none -> 20.2 us  [expand_skins_in(): array_here = jax.lax.psum(array_here, dev_i)]
  transfers between devices with their start and end apart: 6 -> 7, of which waited for: 4 -> 6; matrix products, arithmetic and copies ran while one was open for 0% -> 2% of each run, Pallas kernels for 0% -> 0%
where the time goes in v1:
time: 412 us; the launch traced here: 411 us
  waiting for transfers between devices  321 us (78%)
  matrix products  34 us (8%)
  blocking collectives  27.7 us (7%)
  between operations  14.9 us (4%)
  local copies, waits for them, and re-layouts  7.4 us (2%)
  other arithmetic  6.04 us (1%)
    reduce_scatter x1, waiting for transfers between devices, shards(): lax.psum_scatter(lax.dot_general(mixed, basis_block, (((0,), (1,)), ((),...  136 us
    all_gather x1, waiting for transfers between devices, shards(): mixed = lax.all_gather(mixed, 'row', axis=0, tiled=True)  83.2 us
    all_gather x1, waiting for transfers between devices, shards(): lax.all_gather(basis_out, ('tp', 'row'), axis=0, tiled=True)  51.4 us
    psum x1, blocking collectives, expand_skins_in(): array_here = jax.lax.psum(array_here, dev_i)  25.6 us
    dot_general x1, matrix products, shards(): lax.dot_general(mixed, basis_block, (((0,), (1,)), ((), ())), preferred_e...  22 us
    all_gather x1, waiting for transfers between devices, shards(): basis_block = lax.all_gather(basis_in, 'col', axis=0, tiled=True)  20.7 us
    psum x1, waiting for transfers between devices, expand_skins_in(): array_here = jax.lax.psum(array_here, dev_i)  20.2 us
    reduce_scatter x1, waiting for transfers between devices, shards(): lax.psum_scatter(mixed_part.astype(jnp.bfloat16), 'col', scatter_dimensio...  8.47 us
  transfers between devices with their start and end apart: 7, of which 6 were waited for; matrix products, arithmetic and copies ran while one was open for 2% of the time, Pallas kernels for 0%

profile of v1, /device:TPU:0, one launch (start us, length us, event | category | flops | bytes accessed | tf_op | source)
XLA Modules:
  0.0 411.4 jit_solution(9068211041737583419)
XLA Ops:
  7.4 0.0 copy-start
  7.4 0.0 all-gather.4.cloned.1.call-start
  7.4 0.7 all-gather.4.cloned.1.call-update
  8.1 0.0 all-reduce.3.cloned.1.call-start
  8.1 1.9 fusion.9
  10.0 0.0 all-reduce.3.cloned.1.call-update
  10.0 0.0 copy-start.1
  10.1 0.0 reduce-scatter.4.cloned.1.call-start
  10.1 20.7 %all-gather.4.cloned.1.call-done = bf16[3584,1024]{1,0:T(8,128)(2,1)} async-done(((bf16[1792,1024]{1,0:T(8,128)(2,1)}), bf16[3584,1024]{1,0:T(8,128)(2,1)}) %all-gather.4.cloned.1.call-update) | async-done | bytes 7340048 | tf_op jit(solution)/shard_map/all_gather | solution.py:30
  30.8 0.0 copy-done
  30.8 5.1 %convolution_convert_fusion.2 = bf16[64,1024]{1,0:T(8,128)(2,1)} fusion(bf16[64,3584]{1,0:T(8,128)(2,1)S(1)} %copy-done, bf16[3584,1024]{1,0:T(8,128)(2,1)} %all-gather.4.cloned.1.call-done), kind=kOutput, calls=%fused_computation.4 | convolution fusion | flops 469827584 | bytes 7929856 | tf_op jit(solution)/shard_map/dot_general | solution.py:31
  35.9 0.0 reduce-scatter.4.cloned.1.call-update
  35.9 0.0 all-gather.6.cloned.1.call-start
  36.0 0.5 all-gather.6.cloned.1.call-update
  36.5 0.0 reduce-scatter.6.cloned.1.call-start
  36.6 20.2 %all-reduce.3.cloned.1.call-done = f32[128,512]{1,0:T(8,128)} async-done(((f32[128,512]{1,0:T(8,128)}), f32[128,512]{1,0:T(8,128)}) %all-reduce.3.cloned.1.call-update) | async-done | bytes 262160 | tf_op jit(solution)/shard_map/psum | solution.py:25
  56.7 25.6 %all-reduce.4 = bf16[128,512]{1,0:T(8,128)(2,1)S(1)} all-reduce(f32[128,512]{1,0:T(8,128)} %all-reduce.3.cloned.1.call-done), channel_id=1, replica_groups=mesh['tp'=4,'row'=4,'col'=2] {'row'}, use_global_device_ids=true, to_apply=%region_2.0 | all-reduce | flops 65536 | bytes 393216 | tf_op jit(solution)/shard_map/psum | solution.py:25
  82.3 0.0 reduce-scatter.4.cloned.1.call-done
  82.4 2.1 all_gather.13
  84.4 51.4 %all-gather.6.cloned.1.call-done = bf16[4096,512]{1,0:T(8,128)(2,1)} async-done(((bf16[256,512]{1,0:T(8,128)(2,1)}), bf16[4096,512]{1,0:T(8,128)(2,1)}) %all-gather.6.cloned.1.call-update) | async-done | bytes 4194320 | tf_op jit(solution)/shard_map/all_gather | solution.py:41
  135.9 0.0 copy-done.1
  135.9 4.9 %convolution_convert_fusion.1 = bf16[256,4096]{1,0:T(8,128)(2,1)} fusion(bf16[4096,512]{1,0:T(8,128)(2,1)} %all-gather.6.cloned.1.call-done, bf16[128,256]{1,0:T(8,128)(2,1)S(1)} %all_gather.13, f32[256,512]{1,0:T(8,128)S(1)} %copy-done.1, bf16[128,512]{1,0:T(8,128)(2,1)S(1)} %all-reduce.4), kind=kOutput, calls=%fused_computation.1 | convolution fusion | flops 1108869120 | bytes 7012352 | tf_op jit(solution)/shard_map/dot_general | solution.py:16
  140.8 3.3 convert_element_type.30
  144.1 4.1 copy.6
  148.2 0.0 reduce-scatter.6.cloned.1.call-update
  148.2 0.0 all-gather.8.cloned.1.call-start
  148.3 8.5 %reduce-scatter.6.cloned.1.call-done = bf16[256,4,1,512]{0,3,1,2:T(8,128)(2,1)} async-done(((bf16[256,4,2,512]{0,3,1,2:T(8,128)(2,1)}), bf16[256,4,1,512]{0,3,1,2:T(8,128)(2,1)}) %reduce-scatter.6.cloned.1.call-update) | async-done | bytes 1048592 | tf_op jit(solution)/shard_map/reduce_scatter | solution.py:45
  156.8 0.0 all-gather.8.cloned.1.call-update
  156.8 0.0 reduce-scatter.8.cloned.1.call-start
  156.8 83.2 %all-gather.8.cloned.1.call-done = bf16[1024,2048]{0,1:T(8,128)(2,1)} async-done(((bf16[256,2048]{0,1:T(8,128)(2,1)}), bf16[1024,2048]{0,1:T(8,128)(2,1)}) %all-gather.8.cloned.1.call-update) | async-done | bytes 4194320 | tf_op jit(solution)/shard_map/all_gather | solution.py:49
  240.0 22.0 %convolution_convert_fusion = bf16[2048,3584]{1,0:T(8,128)(2,1)} fusion(bf16[1024,2048]{0,1:T(8,128)(2,1)} %all-gather.8.cloned.1.call-done, bf16[3584,1024]{1,0:T(8,128)(2,1)} %all-gather.4.cloned.1.call-done), kind=kOutput, calls=%fused_computation | convolution fusion | flops 15039725568 | bytes 26214400 | tf_op jit(solution)/shard_map/dot_general | solution.py:51
  262.0 0.0 reduce-scatter.8.cloned.1.call-update
  262.1 135.9 %reduce-scatter.8.cloned.1.call-done = bf16[512,3584]{1,0:T(8,128)(2,1)} async-done(((bf16[2048,3584]{1,0:T(8,128)(2,1)}), bf16[512,3584]{1,0:T(8,128)(2,1)}) %reduce-scatter.8.cloned.1.call-update) | async-done | bytes 3670032 | tf_op jit(solution)/shard_map/reduce_scatter | solution.py:50
  398.0 6.0 %convert_element_type.33 = f32[512,3584]{1,0:T(8,128)} convert(bf16[512,3584]{1,0:T(8,128)(2,1)} %reduce-scatter.8.cloned.1.call-done) | non-fusion elementwise | flops 1835008 | bytes 11010048 | tf_op jit(solution)/shard_map/convert_element_type | solution.py:57
Async XLA Ops:
  7.4 23.4 %copy-start = (bf16[64,3584]{1,0:T(8,128)(2,1)S(1)}, bf16[64,3584]{1,0:T(8,128)(2,1)}, u32[]{:S(2)}) copy-start(bf16[64,3584]{1,0:T(8,128)(2,1)} %param.5) | copy-start | bytes 1376260
  7.4 23.4 %all-gather.4.cloned.1.call-start = ((), (), s32[]{:S(2)}) async-start(), calls=%async_computation.3 | async-start | bytes 11010048 | tf_op jit(solution)/shard_map/all_gather | solution.py:30
  8.1 48.7 %all-reduce.3.cloned.1.call-start = ((), (), s32[]{:S(2)}) async-start(), calls=%async_computation.5 | async-start | bytes 524288 | tf_op jit(solution)/shard_map/psum | solution.py:25
  10.0 125.8 %copy-start.1 = (f32[256,512]{1,0:T(8,128)S(1)}, f32[256,512]{1,0:T(8,128)}, u32[]{:S(2)}) copy-start(f32[256,512]{1,0:T(8,128)} %param.9) | copy-start | bytes 1572868
  10.1 72.3 %reduce-scatter.4.cloned.1.call-start = ((), (), s32[]{:S(2)}) async-start(), calls=%async_computation.4 | async-start | bytes 163840 | tf_op jit(solution)/shard_map/reduce_scatter | solution.py:32
  35.9 100.0 %all-gather.6.cloned.1.call-start = ((), (), s32[]{:S(2)}) async-start(), calls=%async_computation.6 | async-start | bytes 4456448 | tf_op jit(solution)/shard_map/all_gather | solution.py:41
  36.5 120.2 %reduce-scatter.6.cloned.1.call-start = ((), (), s32[]{:S(2)}) async-start(), calls=%async_computation.7 | async-start | bytes 3145728 | tf_op jit(solution)/shard_map/reduce_scatter | solution.py:45
  148.2 91.8 %all-gather.8.cloned.1.call-start = ((), (), s32[]{:S(2)}) async-start(), calls=%async_computation.8 | async-start | bytes 5242880 | tf_op jit(solution)/shard_map/all_gather | solution.py:49
  156.8 241.2 %reduce-scatter.8.cloned.1.call-start = ((), (), s32[]{:S(2)}) async-start(), calls=%async_computation.9 | async-start | bytes 18350080 | tf_op jit(solution)/shard_map/reduce_scatter | solution.py:50
Sparse Core Ops, SparseCore 0:
  9.7 21.0 all-gather.3
  36.1 20.6 reduce-scatter.3
  148.4 8.3 reduce-scatter.5
  158.2 81.8 all-gather.7
Sparse Core Ops, SparseCore 1:
  11.5 45.2 all-reduce.2
  59.4 76.5 all-gather.5
  262.1 135.8 reduce-scatter.7
